TPU v7x, 256 devices: a whole 4x4x8 slice. The times are simulated.
256 devices in a mesh: row: 16 (over z, core), col: 8 (over x, y_lo), vec: 2 (over y_hi).
Axes of the slice: x: 4, y: 4 (y_hi: 2, y_lo: 2; y = y_hi * 2 + y_lo), z: 8, core: 2. Of those that a mesh axis runs over, the one named last changes fastest.
Arguments:
- vectors: bfloat16 [16, 131072], P('vec', ('row', 'col')), may hold values from -6 to 6
- tile_vals: bfloat16 [16, 8, 256, 128, 128], P('row', 'col'), may hold values from -0.09375 to 0.09375
- tile_rows: int32 [16, 8, 256], P('row', 'col'), may hold values from 0 to 1023, as said below
- tile_cols: int32 [16, 8, 256], P('row', 'col'), may hold values from 0 to 1023, as said below
- tile_counts: int32 [16, 8], P('row', 'col'), may hold values from 1 to 256, as said below
Outputs:
- product: bfloat16 [16, 131072], P('vec', ('row', 'col'))
- gram: float32 [16, 16], P(None, 'vec')
Inputs may be any that keep to these rules, and one draw needn't show every extreme that they name: `tile_rows`: list [i, j] names tiles whose row index r has i * 64 <= r < (i + 1) * 64 and whose column index c has (c // 8) % (8) == j, that is the column's block of 8 tile rows, numbered c // 8, is held by column group j; live slots name distinct tiles with r >= c; slots at or beyond the count hold in-range indices that must be ignored. `tile_cols`: see tile_rows; the same slots. `tile_counts`: some lists are full in every draw; lists near the top of the triangle hold few tiles.
All inputs are finite; a program needn't handle non-finite values.
Results may differ from a plain program's by a relative error of at most 0.001.
Values may be sent and summed in bfloat16 or wider, within the bound.
A program may use at most 64 MiB of HBM per device.

v0:
```python
import math

import jax
import jax.numpy as jnp
from jax import lax
from jax.sharding import PartitionSpec as P


def shards(vectors, tile_vals, tile_rows, tile_cols, tile_counts):
    nrow = lax.axis_size("row")
    ncol = lax.axis_size("col")
    vlocal, width = vectors.shape
    tile = tile_vals.shape[-1]
    stretch = width // tile
    span = ncol * stretch
    colspan = nrow * stretch
    row_x = lax.all_gather(vectors, "col", axis=1, tiled=True)
    col_x = lax.all_gather(vectors, "row", axis=1, tiled=True)
    tiles = tile_vals[0, 0]
    rows = tile_rows[0, 0]
    cols = tile_cols[0, 0]
    count = tile_counts[0, 0]
    slots = jnp.arange(rows.shape[0], dtype=jnp.int32)
    live = slots < count
    mirror = live & (rows != cols)
    row_place = rows % span
    col_place = cols // span * stretch + cols % stretch
    row_blocks = row_x.reshape(vlocal, span, tile)
    col_blocks = col_x.reshape(vlocal, colspan, tile)
    picked_cols = jnp.take(col_blocks, col_place, axis=1)
    picked_rows = jnp.take(row_blocks, row_place, axis=1)
    down = jnp.einsum("tij,vtj->vti", tiles, picked_cols, preferred_element_type=jnp.float32)
    upper = jnp.einsum("tij,vti->vtj", tiles, picked_rows, preferred_element_type=jnp.float32)
    row_hit = (
        (row_place[None, :] == jnp.arange(span, dtype=jnp.int32)[:, None]) & live[None, :]
    ).astype(jnp.float32)
    col_hit = (
        (col_place[None, :] == jnp.arange(colspan, dtype=jnp.int32)[:, None]) & mirror[None, :]
    ).astype(jnp.float32)
    row_part = jnp.einsum("at,vti->vai", row_hit, down, precision=lax.Precision.HIGHEST).reshape(
        vlocal, span * tile
    )
    col_part = jnp.einsum("at,vti->vai", col_hit, upper, precision=lax.Precision.HIGHEST).reshape(
        vlocal, colspan * tile
    )
    row_whole = lax.psum(row_part, "col")
    col_whole = lax.psum(col_part, "row")
    row_share = lax.dynamic_slice_in_dim(row_whole, lax.axis_index("col") * width, width, 1)
    col_share = lax.dynamic_slice_in_dim(col_whole, lax.axis_index("row") * width, width, 1)
    image = row_share + col_share
    every_vector = lax.all_gather(vectors, "vec", axis=0, tiled=True)
    partial_gram = jnp.dot(
        every_vector.astype(jnp.float32), image.T, precision=lax.Precision.HIGHEST
    )
    gram = lax.psum(partial_gram, ("row", "col")) / math.sqrt(width * nrow * ncol)
    return (image.astype(jnp.bfloat16), gram)


def solution(mesh):
    return jax.shard_map(
        shards,
        mesh=mesh,
        in_specs=(
            P("vec", ("row", "col")),
            P("row", "col", None, None, None),
            P("row", "col", None),
            P("row", "col", None),
            P("row", "col"),
        ),
        out_specs=(P("vec", ("row", "col")), P(None, "vec")),
        check_vma=False,
    )
```

profile of v0, /device:TPU:8, one launch (start us, length us, event | category | flops | bytes accessed | tf_op | source)
XLA Modules:
  0.0 527.4 jit_solution(8425430569256399796)
XLA Ops:
  7.2 0.0 copy-start.1
  7.2 0.0 copy-start.2
  7.2 0.0 all-reduce.5.cloned.1.call-start
  7.2 28.5 %all_gather.10 = bf16[8,8192]{1,0:T(8,128)(2,1)S(1)} all-gather(bf16[8,1024]{1,0:T(8,128)(2,1)} %param.5), channel_id=1, replica_groups=mesh['row'=16,'col'=8,'vec'=2] {'col'}, dimensions={1}, use_global_device_ids=true | all-gather | bytes 147456 | tf_op jit(solution)/shard_map/all_gather | solution.py:17
  35.8 0.7 compare_select_fusion
  36.5 0.7 compare_and_fusion.1
  37.2 0.8 gather_fusion.1
  38.0 0.0 copy-start
  38.0 4.7 fusion
  42.7 0.4 copy.9
  43.8 0.0 copy-done.1
  43.8 0.0 copy-done.2
  43.8 0.6 convolution_bitcast_fusion
  44.5 0.2 copy.7
  44.7 1.1 copy.18
  45.8 0.0 all-reduce.5.cloned.1.call-update
  45.8 0.0 all-reduce.3.cloned.1.call-start
  45.9 0.0 copy-done
  45.9 20.7 %all_gather.9 = bf16[8,16384]{1,0:T(8,128)(2,1)S(1)} all-gather(bf16[8,1024]{1,0:T(8,128)(2,1)S(1)} %copy-done), channel_id=1, replica_groups=mesh['row'=16,'col'=8,'vec'=2] {'row'}, dimensions={1}, use_global_device_ids=true | all-gather | bytes 278528 | tf_op jit(solution)/shard_map/all_gather | solution.py:18
  66.6 0.8 gather_fusion
  67.4 6.8 %fusion.2 = f32[256,8,128]{2,1,0:T(8,128)S(1)} fusion(bf16[1,1,256,128,128]{4,3,2,1,0:T(8,128)(2,1)} %param.6, bf16[256,8,128]{2,1,0:T(8,128)(2,1)S(1)} %gather_fusion, pred[256]{0:T(512)(128)(4,1)S(1)} %get-tuple-element.2), kind=kOutput, calls=%fused_computation.4 | convolution fusion | flops 67371008 | bytes 9961728 | tf_op jit(solution)/shard_map/tij,vtj->vti/dot_general | solution.py:32
  74.2 0.6 convolution_bitcast_fusion.1
  74.8 0.9 copy.19
  75.7 0.0 all-reduce.3.cloned.1.call-update
  75.7 5.9 %all_gather.11 = bf16[16,1024]{1,0:T(8,128)(2,1)S(1)} all-gather(bf16[8,1024]{1,0:T(8,128)(2,1)S(1)} %copy-done), channel_id=1, replica_groups=mesh['row'=16,'col'=8,'vec'=2] {'vec'}, dimensions={0}, use_global_device_ids=true | all-gather | bytes 49152 | tf_op jit(solution)/shard_map/all_gather | solution.py:51
  81.7 77.3 %all-reduce.5.cloned.1.call-done = f32[8,16384]{1,0:T(8,128)} async-done(((f32[8,16384]{1,0:T(8,128)}), f32[8,16384]{1,0:T(8,128)}) %all-reduce.5.cloned.1.call-update) | async-done | bytes 524304 | tf_op jit(solution)/shard_map/psum | solution.py:47
  159.0 79.9 %all-reduce.3.cloned.1.call-done = f32[8,8192]{1,0:T(8,128)} async-done(((f32[8,8192]{1,0:T(8,128)}), f32[8,8192]{1,0:T(8,128)}) %all-reduce.3.cloned.1.call-update) | async-done | bytes 262160 | tf_op jit(solution)/shard_map/psum | solution.py:46
  238.9 0.9 convolution_bitcast_fusion.2
  239.8 278.8 %psum.23 = f32[16,8]{0,1:T(8,128)S(1)} all-reduce(f32[16,8]{0,1:T(8,128)S(1)} %convolution_bitcast_fusion.2), channel_id=1, replica_groups=mesh['row'=16,'col'=8,'vec'=2] {'row','col'}, use_global_device_ids=true, to_apply=%region_2.3 | all-reduce | flops 128 | bytes 1024 | tf_op jit(solution)/shard_map/psum | solution.py:55
  518.6 0.6 broadcast_multiply_fusion
  519.2 1.4 fusion.25
  (5 shorter events, 0.1 us)
Async XLA Ops:
  7.2 36.6 %copy-start.1 = (s32[1,1,256]{2,1,0:T(1,128)S(1)}, s32[1,1,256]{2,1,0:T(1,128)}, u32[]{:S(2)}) copy-start(s32[1,1,256]{2,1,0:T(1,128)} %param.7) | copy-start | bytes 3076
  7.2 36.6 %copy-start.2 = (s32[1,1,256]{2,1,0:T(1,128)S(1)}, s32[1,1,256]{2,1,0:T(1,128)}, u32[]{:S(2)}) copy-start(s32[1,1,256]{2,1,0:T(1,128)} %param.8) | copy-start | bytes 3076
  7.2 151.8 %all-reduce.5.cloned.1.call-start = ((), (), s32[]{:S(2)}) async-start(), calls=%async_computation.1 | async-start | bytes 1048576 | tf_op jit(solution)/shard_map/psum | solution.py:47
  38.0 7.9 %copy-start = (bf16[8,1024]{1,0:T(8,128)(2,1)S(1)}, bf16[8,1024]{1,0:T(8,128)(2,1)}, u32[]{:S(2)}) copy-start(bf16[8,1024]{1,0:T(8,128)(2,1)} %param.5) | copy-start | bytes 49156
  45.8 193.1 %all-reduce.3.cloned.1.call-start = ((), (), s32[]{:S(2)}) async-start(), calls=%async_computation | async-start | bytes 524288 | tf_op jit(solution)/shard_map/psum | solution.py:46
Sparse Core Ops, SparseCore 0:
  45.9 112.9 all-reduce.4
  161.6 77.2 all-reduce.2
where the time goes:
time: 528 us; the launch traced here: 527 us
  blocking collectives  334 us (63%)
  waiting for transfers between devices  157 us (30%)
  between operations  14.8 us (3%)
  matrix products  13.7 us (3%)
    psum x1, blocking collectives, shards(): lax.psum(partial_gram, ('row', 'col')) / math.sqrt(width * nrow * ncol)  279 us
    psum x1, waiting for transfers between devices, shards(): row_whole = lax.psum(row_part, 'col')  79.9 us
    psum x1, waiting for transfers between devices, shards(): col_whole = lax.psum(col_part, 'row')  77.3 us
    all_gather x1, blocking collectives, shards(): row_x = lax.all_gather(vectors, 'col', axis=1, tiled=True)  28.5 us
    all_gather x1, blocking collectives, shards(): col_x = lax.all_gather(vectors, 'row', axis=1, tiled=True)  20.7 us
  transfers between devices with their start and end apart: 2, of which 2 were waited for; matrix products, arithmetic and copies ran while one was open for 2% of the time, Pallas kernels for 0%

commit v1 on v0

v1 whole, which is shorter than its diff:
```python
import functools
import math

import jax
import jax.numpy as jnp
from jax import lax
from jax.experimental import pallas as pl
from jax.experimental.pallas import tpu as pltpu
from jax.sharding import PartitionSpec as P

MESH = pl.DeviceIdType.MESH
BF16 = jnp.bfloat16
F32 = jnp.float32
CHUNKS = 8


def split_hi_lo(value):
    hi = value.astype(BF16)
    lo = (value - hi.astype(F32)).astype(BF16)
    return hi, lo


def kernel(
    n_row, n_col, scale,
    rows_s, cols_s, count_s, rows_v, cols_v, x_ref, tiles_hbm,
    prod_ref, gram_ref,
    tiles, x_mine, x_row, x_oth, x_col, upper, down, col_part, exch, z_acc, z_recv, row_part, row_recv, acc,
    g1_send, g1_recv, g2_send, g2_recv,
    tile_sem, mine_sem, xz_s, xz_r, xf_s, xf_r, xr_s, xr_r, xo_s, xo_r, ex_s, ex_r, zs_s, zs_r, rs_s, rs_r,
    g1_s, g1_r, g2_s, g2_r,
):
    n_z = n_row // 2
    slots = tiles.shape[0]
    tile = tiles.shape[1]
    vloc = x_ref.shape[0]
    ch = x_ref.shape[1] // tile
    blk = ch * vloc
    span = n_col * ch
    per = slots // CHUNKS
    span_bits = span.bit_length() - 1
    row = lax.axis_index("row")
    col = lax.axis_index("col")
    vec = lax.axis_index("vec")
    z = row // 2
    core = row % 2
    oth = 1 - vec

    def tile_copy(c):
        part = pl.ds(c * per, per)
        return pltpu.make_async_copy(tiles_hbm.at[0, 0, part], tiles.at[part], tile_sem.at[c])

    def mine_copy(m):
        return pltpu.make_async_copy(x_ref.at[:, pl.ds(m * tile, tile)], x_mine.at[m], mine_sem.at[m])

    for m in range(ch):
        mine_copy(m).start()
    for c in range(CHUNKS):
        tile_copy(c).start()

    barrier = pltpu.get_barrier_semaphore()
    for d in range(1, n_row):
        pl.semaphore_signal(barrier, inc=1, device_id={"row": (row + d) % n_row}, device_id_type=MESH)
    for d in range(1, n_col):
        pl.semaphore_signal(barrier, inc=1, device_id={"col": (col + d) % n_col}, device_id_type=MESH)
    for d in range(n_col):
        pl.semaphore_signal(barrier, inc=1, device_id={"col": (col + d) % n_col, "vec": oth}, device_id_type=MESH)
    for m in range(ch):
        mine_copy(m).wait()
    pl.semaphore_wait(barrier, n_row - 1 + 2 * n_col - 1)

    def remote(src, dst, send, recv, to):
        return pltpu.make_async_remote_copy(
            src_ref=src, dst_ref=dst, send_sem=send, recv_sem=recv, device_id=to, device_id_type=MESH
        )

    far = sorted(range(1, n_z), key=lambda d: -min(d, n_z - d))

    def owned(k):
        return pl.ds(k * ch, ch)

    def x_up(d):
        return remote(x_mine, x_col.at[owned(row)], xz_s.at[d], xz_r.at[z], {"row": (row + 2 * d) % n_row})

    def x_side(d):
        return remote(x_mine, x_row.at[owned(col)], xr_s.at[d], xr_r.at[col], {"col": (col + d) % n_col})

    def x_over(d):
        return remote(
            x_mine, x_oth.at[owned(col)], xo_s.at[d], xo_r.at[col], {"col": (col + d) % n_col, "vec": oth}
        )

    for d in far:
        @pl.when(z + d < n_z)
        def _():
            x_up(d).start()
    for d in range(1, n_col):
        x_side(d).start()
    x_row[owned(col)] = x_mine[...]
    x_col[owned(row)] = x_mine[...]
    for k in range(2, n_row):
        @pl.when(k // 2 > z)
        def _():
            x_col[owned(k)] = jnp.zeros((ch, vloc, tile), BF16)
    count = count_s[0, 0]
    slot_iota = lax.broadcasted_iota(jnp.int32, (1, slots), 1)
    live = slot_iota < count
    rows_l = rows_v[0]
    cols_l = cols_v[0]

    mate = {"row": row + 1 - 2 * core}

    def x_mate():
        return remote(x_mine, x_col.at[owned(row)], xf_s.at[n_z], xf_r.at[n_z], mate)

    def x_forward(zz):
        part = x_col.at[owned(2 * zz + core)]
        return remote(part, part, xf_s.at[zz], xf_r.at[zz], mate)

    x_mate().start()

    def recv_wait(dst, sem):
        pltpu.make_async_copy(dst, dst, sem).wait()

    for d in range(1, n_col):
        src = (col + d) % n_col
        recv_wait(x_row.at[owned(src)], xr_r.at[src])
    for d in range(n_col):
        x_over(d).start()

    zero = jnp.zeros((2 * vloc, tile), BF16)

    def four(pick, first, out, trans):
        xs = [pick(first + q) for q in range(4)]
        a = [tiles[first + q] for q in range(4)]
        top = jnp.concatenate([xs[0], xs[1]], 0)
        bot = jnp.concatenate([xs[2], xs[3]], 0)
        left = jnp.concatenate([jnp.concatenate([top, zero], 0), jnp.concatenate([zero, bot], 0)], 1)
        if trans:
            w = jnp.concatenate([jnp.concatenate([a[0], a[1]], 0), jnp.concatenate([a[2], a[3]], 0)], 1)
            dims = (((1,), (1,)), ((), ()))
        else:
            w = jnp.concatenate([jnp.concatenate([a[0], a[1]], 1), jnp.concatenate([a[2], a[3]], 1)], 0)
            dims = (((1,), (0,)), ((), ()))
        r = lax.dot_general(left, w, dims, preferred_element_type=F32)
        base = pl.multiple_of(first * vloc, 4 * vloc)
        for q in range(4):
            side = q % 2
            out[pl.ds(base + q * vloc, vloc), :] = r[q * vloc:(q + 1) * vloc, side * tile:(side + 1) * tile]

    def pick_row(t):
        return x_row[rows_s[0, 0, t] & (span - 1)]

    def pick_col(t):
        c = cols_s[0, 0, t]
        return x_col[lax.shift_right_logical(c, span_bits) * ch + (c & (ch - 1))]

    def up_step(c, carry):
        tile_copy(c).wait()
        for q in range(per // 4):
            four(pick_row, c * per + 4 * q, upper, False)
        return carry

    lax.fori_loop(0, CHUNKS, up_step, 0)

    for d in far:
        @pl.when(z - d >= 0)
        def _():
            recv_wait(x_col.at[owned(2 * (z - d) + core)], xz_r.at[z - d])
            x_forward(z - d).start()

    def scatter(src, hot, dst):
        m = hot.shape[0]
        for p in range(vloc // 2):
            both = jnp.concatenate(
                [src[pl.ds(2 * p, slots, stride=vloc), :], src[pl.ds(2 * p + 1, slots, stride=vloc), :]], 1
            )
            hi, lo = split_hi_lo(both)
            res = jnp.dot(hot, hi, preferred_element_type=F32) + jnp.dot(hot, lo, preferred_element_type=F32)
            dst[pl.ds(2 * p, m, stride=vloc), :] = res[:, :tile]
            dst[pl.ds(2 * p + 1, m, stride=vloc), :] = res[:, tile:]

    def one_hot(place, m):
        hit = lax.broadcasted_iota(jnp.int32, (m, slots), 0) == place
        return jnp.where(hit, 1.0, 0.0).astype(BF16)

    group = cols_l // span
    col_place = (group % 2) * (n_z * ch) + (group // 2) * ch + cols_l % ch
    scatter(upper, one_hot(jnp.where(live & (rows_l != cols_l), col_place, -1), n_row * ch), col_part)

    half = n_z * blk
    swap = remote(
        col_part.at[pl.ds(pl.multiple_of((1 - core) * half, blk), half)], exch, ex_s, ex_r, mate
    )
    swap.start()

    recv_wait(x_col.at[owned(row + 1 - 2 * core)], xf_r.at[n_z])
    for d in far:
        @pl.when(z - d >= 0)
        def _():
            recv_wait(x_col.at[owned(2 * (z - d) + 1 - core)], xf_r.at[z - d])

    def down_step(c, carry):
        for q in range(per // 4):
            four(pick_col, c * per + 4 * q, down, True)
        return carry

    lax.fori_loop(0, CHUNKS // 2, down_step, 0)

    recv_wait(exch, ex_r)

    def z_block(zz):
        return pl.ds(pl.multiple_of(zz * blk, blk), blk)

    def z_send(d):
        return remote(
            z_acc.at[z_block(z - d)], z_recv.at[z], zs_s.at[d], zs_r.at[z], {"row": row - 2 * d}
        )

    mine = pl.multiple_of(core * half, blk)
    z_acc[...] = col_part[pl.ds(mine, half), :] + exch[...]
    for d in far:
        @pl.when(z - d >= 0)
        def _():
            z_send(d).start()

    lax.fori_loop(CHUNKS // 2, CHUNKS, down_step, 0)

    row_hot = jnp.concatenate(
        [
            one_hot(jnp.where(live, rows_l % span, -1), span),
            one_hot(jnp.where(live & (rows_l == cols_l), rows_l % ch, -1), 2 * ch),
        ],
        0,
    )
    scatter(down, row_hot, row_part)

    def r_send(d):
        to = (col + d) % n_col
        return remote(
            row_part.at[pl.ds(pl.multiple_of(to * blk, blk), blk)], row_recv.at[col], rs_s.at[d], rs_r.at[col],
            {"col": to},
        )

    for d in range(1, n_col):
        r_send(d).start()

    for d in range(n_col):
        recv_wait(x_oth.at[owned((col + d) % n_col)], xo_r.at[(col + d) % n_col])

    def against(base, j):
        part = jnp.concatenate(
            [row_part[pl.ds(base + m * vloc, vloc), :] for m in range(ch)], 1
        )
        hi, lo = split_hi_lo(part)
        left = jnp.concatenate([hi, lo], 0)
        right = jnp.concatenate(
            [
                jnp.concatenate([x[j * ch + m] for m in range(ch)], 1)
                for x in (x_row, x_oth)
            ],
            0,
        )
        r = lax.dot_general(left, right, (((1,), (1,)), ((), ())), preferred_element_type=F32)
        return r[:vloc] + r[vloc:]

    whole = against(0, 0)
    for jj in range(1, n_col):
        whole = whole + against(jj * blk, jj)
    off = whole - against(span * vloc, col)
    pad = jnp.zeros((vloc, tile - 4 * vloc), F32)
    g1_send[...] = jnp.concatenate([off, whole, pad], 1)

    def g1_side(d):
        return remote(g1_send, g1_recv.at[vec, col], g1_s.at[vec, d], g1_r.at[vec, col], {"col": (col + d) % n_col})

    def g1_over(d):
        return remote(
            g1_send, g1_recv.at[vec, col], g1_s.at[oth, d], g1_r.at[vec, col],
            {"col": (col + d) % n_col, "vec": oth},
        )

    for d in range(n_col):
        g1_over(d).start()
    for d in range(1, n_col):
        g1_side(d).start()

    image = row_part[pl.ds(pl.multiple_of(col * blk, blk), blk), :]
    for d in range(1, n_col):
        src = (col + d) % n_col
        recv_wait(row_recv.at[src], rs_r.at[src])
        image = image + row_recv[src]
    acc[...] = image + z_acc[z_block(z), :]

    own = g1_send[...]
    for d in range(1, n_col):
        src = (col + d) % n_col
        recv_wait(g1_recv.at[vec, src], g1_r.at[vec, src])
        own = own + g1_recv[vec, src]
    other = None
    for d in range(n_col):
        src = (col + d) % n_col
        recv_wait(g1_recv.at[oth, src], g1_r.at[oth, src])
        other = g1_recv[oth, src] if other is None else other + g1_recv[oth, src]
    lane = lax.broadcasted_iota(jnp.int32, (vloc, tile), 1)
    own = jnp.where(lane < 4 * vloc, own, pltpu.roll(other, 4 * vloc, 1))
    g2_send[...] = own

    def g2(d):
        return remote(g2_send, g2_recv.at[row], g2_s.at[d], g2_r.at[row], {"row": (row + d) % n_row})

    order = sorted(range(1, n_row), key=lambda d: -min(d, n_row - d))
    for d in order:
        g2(d).start()

    for d in range(n_z - 1, 0, -1):
        @pl.when(z + d < n_z)
        def _():
            src = (z + d) % n_z
            recv_wait(z_recv.at[src], zs_r.at[src])
            acc[...] += z_recv[src]

    for m in range(ch):
        prod_ref[:, m * tile:(m + 1) * tile] = acc[m * vloc:(m + 1) * vloc, :].astype(BF16)

    total = own
    for d in range(1, n_row):
        src = (row + d) % n_row
        recv_wait(g2_recv.at[src], g2_r.at[src])
        total = total + g2_recv[src]
    flip = jnp.transpose(total)
    g_own = total[:, :vloc] + flip[2 * vloc:3 * vloc, :]
    g_oth = pltpu.roll(total, tile - 5 * vloc, 1)[:, :vloc] + flip[3 * vloc:4 * vloc, :]
    gram_ref[pl.ds(pl.multiple_of(vec * vloc, vloc), vloc), :] = g_own * scale
    gram_ref[pl.ds(pl.multiple_of(oth * vloc, vloc), vloc), :] = g_oth * scale

    x_mate().wait_send()
    swap.wait_send()
    for d in range(1, n_z):
        @pl.when(z + d < n_z)
        def _():
            x_up(d).wait_send()

        @pl.when(z - d >= 0)
        def _():
            x_forward(z - d).wait_send()
            z_send(d).wait_send()
    for d in range(1, n_col):
        x_side(d).wait_send()
        r_send(d).wait_send()
        g1_side(d).wait_send()
    for d in range(n_col):
        x_over(d).wait_send()
        g1_over(d).wait_send()
    for d in range(1, n_row):
        g2(d).wait_send()


def shards(n_row, n_col, vectors, tile_vals, tile_rows, tile_cols, tile_counts):
    vloc, width = vectors.shape
    slots, tile = tile_vals.shape[2], tile_vals.shape[3]
    ch = width // tile
    blk = ch * vloc
    n_z = n_row // 2
    dma = pltpu.SemaphoreType.DMA
    vmem = functools.partial(pl.BlockSpec, memory_space=pltpu.VMEM)
    smem = functools.partial(pl.BlockSpec, memory_space=pltpu.SMEM)
    scale = 1.0 / math.sqrt(width * n_row * n_col)
    return pl.pallas_call(
        functools.partial(kernel, n_row, n_col, scale),
        out_shape=(
            jax.ShapeDtypeStruct((vloc, width), BF16),
            jax.ShapeDtypeStruct((2 * vloc, vloc), F32),
        ),
        in_specs=[smem(), smem(), smem(), vmem(), vmem(), vmem(), pl.BlockSpec(memory_space=pl.ANY)],
        out_specs=(vmem(), vmem()),
        scratch_shapes=[
            pltpu.VMEM((slots, tile, tile), BF16),
            pltpu.VMEM((ch, vloc, tile), BF16),
            pltpu.VMEM((n_col * ch, vloc, tile), BF16),
            pltpu.VMEM((n_col * ch, vloc, tile), BF16),
            pltpu.VMEM((n_row * ch, vloc, tile), BF16),
            pltpu.VMEM((slots * vloc, tile), F32),
            pltpu.VMEM((slots * vloc, tile), F32),
            pltpu.VMEM((n_row * blk, tile), F32),
            pltpu.VMEM((n_z * blk, tile), F32),
            pltpu.VMEM((n_z * blk, tile), F32),
            pltpu.VMEM((n_z, blk, tile), F32),
            pltpu.VMEM(((n_col + 2) * blk, tile), F32),
            pltpu.VMEM((n_col, blk, tile), F32),
            pltpu.VMEM((blk, tile), F32),
            pltpu.VMEM((vloc, tile), F32),
            pltpu.VMEM((2, n_col, vloc, tile), F32),
            pltpu.VMEM((vloc, tile), F32),
            pltpu.VMEM((n_row, vloc, tile), F32),
            dma((CHUNKS,)), dma((ch,)),
            dma((n_z,)), dma((n_z,)),
            dma((n_z + 1,)), dma((n_z + 1,)),
            dma((n_col,)), dma((n_col,)),
            dma((n_col,)), dma((n_col,)),
            dma(()), dma(()),
            dma((n_z,)), dma((n_z,)),
            dma((n_col,)), dma((n_col,)),
            dma((2, n_col)), dma((2, n_col)),
            dma((n_row,)), dma((n_row,)),
        ],
        compiler_params=pltpu.CompilerParams(
            collective_id=0, has_side_effects=True, vmem_limit_bytes=60 * 1024 * 1024
        ),
    )(tile_rows, tile_cols, tile_counts, tile_rows, tile_cols, vectors, tile_vals)


def solution(mesh):
    return jax.shard_map(
        functools.partial(shards, mesh.shape["row"], mesh.shape["col"]),
        mesh=mesh,
        in_specs=(
            P("vec", ("row", "col")),
            P("row", "col", None, None, None),
            P("row", "col", None),
            P("row", "col", None),
            P("row", "col"),
        ),
        out_specs=(P("vec", ("row", "col")), P(None, "vec")),
        check_vma=False,
    )
```

time: 528 us -> 41.8 us (0.08)
  the two profiles are of different devices: /device:TPU:8 before, /device:TPU:1 now
where the time goes in v1:
time: 41.8 us; the launch traced here: 41.5 us
  Pallas kernels  37.6 us (90%)
  local copies, waits for them, and re-layouts  2.68 us (6%)
  between operations  1.29 us (3%)
    pallas_call x1, Pallas kernels, shards(): pl.pallas_call(functools.partial(kernel, n_row, n_col, scale), out_shape=...  37.6 us
    pallas_call x1, local copies, waits for them, and re-layouts, shards(): pl.pallas_call(functools.partial(kernel, n_row, n_col, scale), out_shape=...  1.36 us
    unnamed x1, local copies, waits for them, and re-layouts  1.32 us

profile of v1, /device:TPU:1, one launch (start us, length us, event | category | flops | bytes accessed | tf_op | source)
XLA Modules:
  0.0 41.5 jit_solution(8119793459099386855)
XLA Ops:
  1.3 37.6 %shard_map.68 = (bf16[8,1024]{1,0:T(8,128)(2,1)}, f32[16,8]{1,0:T(8,128)}) custom-call(s32[1,1,256]{2,1,0:T(1,128)} %rows_v.1, s32[1,1,256]{2,1,0:T(1,128)} %cols_v.1, s32[1,1]{1,0:T(1,128)S(6)} %copy.9.count_s, s32[1,1,256]{2,1,0:T(1,128)} %rows_v.1, s32[1,1,256]{2,1,0:T(1,128)} %cols_v.1, bf16[8,1024]{1,0:T(8,128)(2,1)} %x_ref.1, ...), custom_call_target="tpu_custom_call" | custom-call | tf_op jit(solution)/shard_map/pallas_call | solution.py:368
  38.9 1.4 %copy.7 = f32[16,8]{0,1:T(8,128)} copy(f32[16,8]{1,0:T(8,128)} %get-tuple-element.3) | data formatting | bytes 1024 | tf_op jit(solution)/shard_map/pallas_call | solution.py:368
  40.2 1.3 %copy.10 = bf16[8,1024]{1,0:T(8,128)(2,1)} copy(bf16[8,1024]{1,0:T(8,128)(2,1)} %get-tuple-element.6) | data formatting | bytes 32768

commit v2 on v1

--- a/solution.py
+++ b/solution.py
@@ -22,11 +22,11 @@
 
 def kernel(
     n_row, n_col, scale,
-    rows_s, cols_s, count_s, rows_v, cols_v, x_ref, tiles_hbm,
+    rows_hbm, cols_hbm, count_hbm, x_ref, tiles_hbm,
     prod_ref, gram_ref,
-    tiles, x_mine, x_row, x_oth, x_col, upper, down, col_part, exch, z_acc, z_recv, row_part, row_recv, acc,
+    rows_s, cols_s, count_s, rows_v, cols_v, tiles, x_mine, x_row, x_oth, x_col, upper, down, col_part, exch, z_acc, z_recv, row_part, row_recv, acc,
     g1_send, g1_recv, g2_send, g2_recv,
-    tile_sem, mine_sem, xz_s, xz_r, xf_s, xf_r, xr_s, xr_r, xo_s, xo_r, ex_s, ex_r, zs_s, zs_r, rs_s, rs_r,
+    list_sem, tile_sem, mine_sem, xz_s, xz_r, xf_s, xf_r, xr_s, xr_r, xo_s, xo_r, ex_s, ex_r, zs_s, zs_r, rs_s, rs_r,
     g1_s, g1_r, g2_s, g2_r,
 ):
     n_z = n_row // 2
@@ -52,8 +52,17 @@
     def mine_copy(m):
         return pltpu.make_async_copy(x_ref.at[:, pl.ds(m * tile, tile)], x_mine.at[m], mine_sem.at[m])
 
+    lists = [
+        pltpu.make_async_copy(src, dst, list_sem.at[q])
+        for q, (src, dst) in enumerate(
+            [(rows_hbm, rows_s), (cols_hbm, cols_s), (count_hbm, count_s), (rows_hbm, rows_v), (cols_hbm, cols_v)]
+        )
+    ]
+
     for m in range(ch):
         mine_copy(m).start()
+    for q in lists:
+        q.start()
     for c in range(CHUNKS):
         tile_copy(c).start()
 
@@ -101,6 +110,8 @@
         @pl.when(k // 2 > z)
         def _():
             x_col[owned(k)] = jnp.zeros((ch, vloc, tile), BF16)
+    for q in lists:
+        q.wait()
     count = count_s[0, 0]
     slot_iota = lax.broadcasted_iota(jnp.int32, (1, slots), 1)
     live = slot_iota < count
@@ -241,9 +252,6 @@
             {"col": to},
         )
 
-    for d in range(1, n_col):
-        r_send(d).start()
-
     for d in range(n_col):
         recv_wait(x_oth.at[owned((col + d) % n_col)], xo_r.at[(col + d) % n_col])
 
@@ -283,13 +291,8 @@
         g1_over(d).start()
     for d in range(1, n_col):
         g1_side(d).start()
-
-    image = row_part[pl.ds(pl.multiple_of(col * blk, blk), blk), :]
-    for d in range(1, n_col):
-        src = (col + d) % n_col
-        recv_wait(row_recv.at[src], rs_r.at[src])
-        image = image + row_recv[src]
-    acc[...] = image + z_acc[z_block(z), :]
+    for d in range(1, n_col):
+        r_send(d).start()
 
     own = g1_send[...]
     for d in range(1, n_col):
@@ -312,6 +315,13 @@
     for d in order:
         g2(d).start()
 
+    image = row_part[pl.ds(pl.multiple_of(col * blk, blk), blk), :]
+    for d in range(1, n_col):
+        src = (col + d) % n_col
+        recv_wait(row_recv.at[src], rs_r.at[src])
+        image = image + row_recv[src]
+    acc[...] = image + z_acc[z_block(z), :]
+
     for d in range(n_z - 1, 0, -1):
         @pl.when(z + d < n_z)
         def _():
@@ -328,10 +338,11 @@
         recv_wait(g2_recv.at[src], g2_r.at[src])
         total = total + g2_recv[src]
     flip = jnp.transpose(total)
-    g_own = total[:, :vloc] + flip[2 * vloc:3 * vloc, :]
-    g_oth = pltpu.roll(total, tile - 5 * vloc, 1)[:, :vloc] + flip[3 * vloc:4 * vloc, :]
-    gram_ref[pl.ds(pl.multiple_of(vec * vloc, vloc), vloc), :] = g_own * scale
-    gram_ref[pl.ds(pl.multiple_of(oth * vloc, vloc), vloc), :] = g_oth * scale
+    g_own = total[:, 2 * vloc:3 * vloc] + flip[:vloc, :vloc]
+    g_oth = total[:, 3 * vloc:4 * vloc] + flip[5 * vloc:6 * vloc, :vloc]
+    first = jnp.where(vec == 0, g_own, g_oth)
+    second = jnp.where(vec == 0, g_oth, g_own)
+    gram_ref[...] = jnp.concatenate([first, second], 1) * scale
 
     x_mate().wait_send()
     swap.wait_send()
@@ -363,17 +374,21 @@
     n_z = n_row // 2
     dma = pltpu.SemaphoreType.DMA
     vmem = functools.partial(pl.BlockSpec, memory_space=pltpu.VMEM)
-    smem = functools.partial(pl.BlockSpec, memory_space=pltpu.SMEM)
     scale = 1.0 / math.sqrt(width * n_row * n_col)
-    return pl.pallas_call(
+    product, gram = pl.pallas_call(
         functools.partial(kernel, n_row, n_col, scale),
         out_shape=(
-            jax.ShapeDtypeStruct((vloc, width), BF16),
-            jax.ShapeDtypeStruct((2 * vloc, vloc), F32),
+            pltpu.VMEM((vloc, width), BF16),
+            pltpu.VMEM((vloc, 2 * vloc), F32),
         ),
-        in_specs=[smem(), smem(), smem(), vmem(), vmem(), vmem(), pl.BlockSpec(memory_space=pl.ANY)],
+        in_specs=[pl.BlockSpec(memory_space=pltpu.HBM)] * 5,
         out_specs=(vmem(), vmem()),
         scratch_shapes=[
+            pltpu.SMEM((1, 1, slots), jnp.int32),
+            pltpu.SMEM((1, 1, slots), jnp.int32),
+            pltpu.SMEM((1, 1), jnp.int32),
+            pltpu.VMEM((1, 1, slots), jnp.int32),
+            pltpu.VMEM((1, 1, slots), jnp.int32),
             pltpu.VMEM((slots, tile, tile), BF16),
             pltpu.VMEM((ch, vloc, tile), BF16),
             pltpu.VMEM((n_col * ch, vloc, tile), BF16),
@@ -392,7 +407,7 @@
             pltpu.VMEM((2, n_col, vloc, tile), F32),
             pltpu.VMEM((vloc, tile), F32),
             pltpu.VMEM((n_row, vloc, tile), F32),
-            dma((CHUNKS,)), dma((ch,)),
+            dma((5,)), dma((CHUNKS,)), dma((ch,)),
             dma((n_z,)), dma((n_z,)),
             dma((n_z + 1,)), dma((n_z + 1,)),
             dma((n_col,)), dma((n_col,)),
@@ -406,7 +421,8 @@
         compiler_params=pltpu.CompilerParams(
             collective_id=0, has_side_effects=True, vmem_limit_bytes=60 * 1024 * 1024
         ),
-    )(tile_rows, tile_cols, tile_counts, tile_rows, tile_cols, vectors, tile_vals)
+    )(tile_rows, tile_cols, tile_counts, vectors, tile_vals)
+    return product, gram.T
 
 
 def solution(mesh):

time: 41.8 us -> 36.6 us (0.88)
  Pallas kernels: 37.6 us -> 34 us
  local copies, waits for them, and re-layouts: 2.68 us -> 1.2 us
    pallas_call x1, Pallas kernels: 37.6 us -> 34 us  [shards(): pl.pallas_call(functools.partial(kernel, n_row, n_col, scale), out_shape=...]
    pallas_call x1 -> x0, local copies, waits for them, and re-layouts: 1.36 us -> none  [shards(): pl.pallas_call(functools.partial(kernel, n_row, n_col, scale), out_shape=...]
    unnamed x1 -> x2, local copies, waits for them, and re-layouts: 1.32 us -> 1.2 us
where the time goes in v2:
time: 36.6 us; the launch traced here: 36.5 us
  Pallas kernels  34 us (93%)
  between operations  1.29 us (4%)
  local copies, waits for them, and re-layouts  1.2 us (3%)
    pallas_call x1, Pallas kernels, shards(): pl.pallas_call(functools.partial(kernel, n_row, n_col, scale), out_shape=...  34 us
    unnamed x2, local copies, waits for them, and re-layouts  1.2 us

profile of v2, /device:TPU:1, one launch (start us, length us, event | category | flops | bytes accessed | tf_op | source)
XLA Modules:
  0.0 36.5 jit_solution(15922410854373644026)
XLA Ops:
  1.3 34.0 %shard_map.68 = (bf16[8,1024]{1,0:T(8,128)(2,1)S(1)}, f32[8,16]{1,0:T(8,128)S(1)}) custom-call(s32[1,1,256]{2,1,0:T(1,128)} %rows_hbm.1, s32[1,1,256]{2,1,0:T(1,128)} %cols_hbm.1, s32[1,1]{1,0:T(1,128)S(6)} %copy.11.count_hbm, bf16[8,1024]{1,0:T(8,128)(2,1)} %x_ref.1, bf16[1,1,256,128,128]{4,3,2,1,0:T(8,128)(2,1)} %tiles_hbm.1), custom_call_target="tpu_custom_call" | custom-call | tf_op jit(solution)/shard_map/pallas_call | solution.py:378
  35.3 0.6 %copy.9 = bf16[8,1024]{1,0:T(8,128)(2,1)} copy(bf16[8,1024]{1,0:T(8,128)(2,1)S(1)} %get-tuple-element.6) | data formatting | bytes 32768
  35.9 0.6 %copy.10 = f32[16,8]{0,1:T(8,128)} copy(f32[16,8]{0,1:T(8,128)S(1)} %bitcast.1) | data formatting | bytes 1024

commit v3 on v2

v3 whole, which is shorter than its diff:
```python
import functools
import math

import jax
import jax.numpy as jnp
from jax import lax
from jax.experimental import pallas as pl
from jax.experimental.pallas import tpu as pltpu
from jax.sharding import PartitionSpec as P

MESH = pl.DeviceIdType.MESH
BF16 = jnp.bfloat16
F32 = jnp.float32
CHUNKS = 8


def split_hi_lo(value):
    hi = value.astype(BF16)
    lo = (value - hi.astype(F32)).astype(BF16)
    return hi, lo


def kernel(
    n_row, n_col, scale,
    count_v, rows_hbm, cols_hbm, x_ref, tiles_hbm,
    prod_ref, gram_ref,
    rows_s, cols_s, rows_v, cols_v, tiles, x_mine, x_row, x_oth, x_col, upper, down, col_part, exch, z_acc, z_recv, row_part, row_recv, acc,
    g1_send, g1_recv, g2_send, g2_recv,
    list_sem, mine_sem, tile_sem, x_s, xz_r, xf_r, xr_r, xo_r, z_s, ex_r, zs_r, o_s, rs_r, g1_r, g2_r,
):
    n_z = n_row // 2
    slots = tiles.shape[0]
    tile = tiles.shape[1]
    vloc = x_ref.shape[0]
    ch = x_ref.shape[1] // tile
    blk = ch * vloc
    span = n_col * ch
    per = slots // CHUNKS
    fold = vloc // 2
    span_bits = span.bit_length() - 1
    row = lax.axis_index("row")
    col = lax.axis_index("col")
    vec = lax.axis_index("vec")
    z = row // 2
    core = row % 2
    oth = 1 - vec

    def tile_copy(c):
        part = pl.ds(c * per, per)
        return pltpu.make_async_copy(tiles_hbm.at[0, 0, part], tiles.at[part], tile_sem)

    def mine_copy(m):
        return pltpu.make_async_copy(x_ref.at[:, pl.ds(m * tile, tile)], x_mine.at[m], mine_sem)

    lists = [
        pltpu.make_async_copy(rows_hbm, rows_s, list_sem.at[0]),
        pltpu.make_async_copy(cols_hbm, cols_s, list_sem.at[1]),
        pltpu.make_async_copy(cols_hbm, cols_v, list_sem.at[2]),
        pltpu.make_async_copy(rows_hbm, rows_v, list_sem.at[3]),
    ]

    for m in range(ch):
        mine_copy(m).start()
    for q in lists:
        q.start()
    for c in range(CHUNKS):
        tile_copy(c).start()

    barrier = pltpu.get_barrier_semaphore()
    for d in range(1, n_row):
        pl.semaphore_signal(barrier, inc=1, device_id={"row": (row + d) % n_row}, device_id_type=MESH)
    for d in range(1, n_col):
        pl.semaphore_signal(barrier, inc=1, device_id={"col": (col + d) % n_col}, device_id_type=MESH)
    for d in range(n_col):
        pl.semaphore_signal(barrier, inc=1, device_id={"col": (col + d) % n_col, "vec": oth}, device_id_type=MESH)
    pltpu.make_async_copy(x_mine, x_mine, mine_sem).wait()
    pl.semaphore_wait(barrier, n_row - 1 + 2 * n_col - 1)

    def remote(src, dst, send, recv, to):
        return pltpu.make_async_remote_copy(
            src_ref=src, dst_ref=dst, send_sem=send, recv_sem=recv, device_id=to, device_id_type=MESH
        )

    far = sorted(range(1, n_z), key=lambda d: -min(d, n_z - d))

    def owned(k):
        return pl.ds(k * ch, ch)

    def x_up(d):
        return remote(x_mine, x_col.at[owned(row)], x_s, xz_r, {"row": (row + 2 * d) % n_row})

    def x_side(d):
        return remote(x_mine, x_row.at[owned(col)], x_s, xr_r, {"col": (col + d) % n_col})

    def x_over(d):
        return remote(
            x_mine, x_oth.at[owned(col)], x_s, xo_r, {"col": (col + d) % n_col, "vec": oth}
        )

    for d in far:
        @pl.when(z + d < n_z)
        def _():
            x_up(d).start()
    for d in range(1, n_col):
        x_side(d).start()
    x_row[owned(col)] = x_mine[...]
    x_col[owned(row)] = x_mine[...]
    for k in range(2, n_row):
        @pl.when(k // 2 > z)
        def _():
            x_col[owned(k)] = jnp.zeros((ch, vloc, tile), BF16)
    for q in lists:
        q.wait()
    rows_l = rows_v[0]
    cols_l = cols_v[0]
    live = lax.broadcasted_iota(jnp.int32, (1, slots), 1) < count_v[0:1, 0:1]

    mate = {"row": row + 1 - 2 * core}

    def x_mate():
        return remote(x_mine, x_col.at[owned(row)], x_s, xf_r, mate)

    def x_forward(zz):
        part = x_col.at[owned(2 * zz + core)]
        return remote(part, part, x_s, xf_r, mate)

    x_mate().start()

    def bytes_of(ref, sem):
        pltpu.make_async_copy(ref, ref, sem).wait()

    def by_z(ref, unit, count, sem):
        for k in range(n_z):
            if count(k):
                @pl.when(z == k)
                def _():
                    bytes_of(ref.at[pl.ds(0, count(k) * unit)], sem)

    bytes_of(x_row.at[pl.ds(0, (n_col - 1) * ch)], xr_r)
    for d in range(n_col):
        x_over(d).start()

    zero = jnp.zeros((vloc, tile), BF16)

    def two(pick, first, out, trans):
        left = jnp.concatenate(
            [
                jnp.concatenate([pick(first), zero], 1),
                jnp.concatenate([zero, pick(first + 1)], 1),
            ],
            0,
        )
        w = jnp.concatenate([tiles[first], tiles[first + 1]], 1 if trans else 0)
        dims = (((1,), (1 if trans else 0,)), ((), ()))
        out[first * vloc:(first + 2) * vloc, :] = lax.dot_general(left, w, dims, preferred_element_type=F32)

    def pick_row(t):
        return x_row[rows_s[0, 0, t] & (span - 1)]

    def pick_col(t):
        c = cols_s[0, 0, t]
        return x_col[lax.shift_right_logical(c, span_bits) * ch + (c & (ch - 1))]

    bytes_of(tiles, tile_sem)
    for t in range(0, slots // 2, 2):
        two(pick_row, t, upper, False)

    by_z(x_col, ch, lambda k: k, xz_r)
    for d in far:
        @pl.when(z - d >= 0)
        def _():
            x_forward(z - d).start()

    for t in range(slots // 2, slots, 2):
        two(pick_row, t, upper, False)

    def scatter(src, hot, dst):
        m = hot.shape[0]
        for p in range(vloc // 2):
            both = jnp.concatenate(
                [src[pl.ds(2 * p, slots, stride=vloc), :], src[pl.ds(2 * p + 1, slots, stride=vloc), :]], 1
            )
            hi, lo = split_hi_lo(both)
            res = jnp.dot(hot, hi, preferred_element_type=F32) + jnp.dot(hot, lo, preferred_element_type=F32)
            dst[pl.ds(2 * p, m, stride=vloc), :] = res[:, :tile]
            dst[pl.ds(2 * p + 1, m, stride=vloc), :] = res[:, tile:]

    def one_hot(place, m):
        hit = lax.broadcasted_iota(jnp.int32, (m, slots), 0) == place
        return jnp.where(hit, 1.0, 0.0).astype(BF16)

    group = cols_l // span
    col_place = (group % 2) * (n_z * ch) + (group // 2) * ch + cols_l % ch
    scatter(upper, one_hot(jnp.where(live & (rows_l != cols_l), col_place, -1), n_row * ch), col_part)

    half = n_z * blk

    def z_block(zz):
        return pl.ds(pl.multiple_of(zz * blk, blk), blk)

    def swap(d):
        give = pl.ds(pl.multiple_of((1 - core) * half + (z - d) * blk, blk), blk)
        return remote(col_part.at[give], exch.at[z_block(z - d)], z_s, ex_r, mate)

    near = far + [0]
    for d in near:
        @pl.when(z - d >= 0)
        def _():
            swap(d).start()

    by_z(x_col, ch, lambda k: k + 1, xf_r)

    def z_send(d):
        return remote(
            z_acc.at[z_block(z - d)], z_recv.at[z], z_s, zs_r, {"row": row - 2 * d}
        )

    for t in range(0, slots, 2):
        if t == slots // 4:
            by_z(exch, blk, lambda k: k + 1, ex_r)
            for d in near:
                @pl.when(z - d >= 0)
                def _():
                    keep = pl.ds(pl.multiple_of(core * half + (z - d) * blk, blk), blk)
                    z_acc[z_block(z - d), :] = col_part[keep, :] + exch[z_block(z - d), :]
                    if d:
                        z_send(d).start()
        two(pick_col, t, down, True)

    row_hot = jnp.concatenate(
        [
            one_hot(jnp.where(live, rows_l % span, -1), span),
            one_hot(jnp.where(live & (rows_l == cols_l), rows_l % ch, -1), 2 * ch),
        ],
        0,
    )
    scatter(down, row_hot, row_part)

    def r_send(d):
        to = (col + d) % n_col
        return remote(
            row_part.at[pl.ds(pl.multiple_of(to * blk, blk), blk)], row_recv.at[col], o_s, rs_r,
            {"col": to},
        )

    bytes_of(x_oth, xo_r)

    def against(base, j):
        part = jnp.concatenate(
            [row_part[pl.ds(base + m * vloc, vloc), :] for m in range(ch)], 1
        )
        hi, lo = split_hi_lo(part)
        left = jnp.concatenate([hi, lo], 0)
        right = jnp.concatenate(
            [
                jnp.concatenate([x[j * ch + m] for m in range(ch)], 1)
                for x in (x_row, x_oth)
            ],
            0,
        )
        r = lax.dot_general(left, right, (((1,), (1,)), ((), ())), preferred_element_type=F32)
        return r[:vloc] + r[vloc:]

    whole = against(0, 0)
    for jj in range(1, n_col):
        whole = whole + against(jj * blk, jj)
    off = whole - against(span * vloc, col)
    pad = jnp.zeros((vloc, tile - 4 * vloc), F32)
    wide = jnp.concatenate([off, whole, pad], 1)
    packed = jnp.concatenate([wide[:1], wide[fold:fold + 1]], 0)
    for k in range(1, fold):
        pair = jnp.concatenate([wide[k:k + 1], wide[fold + k:fold + k + 1]], 0)
        packed = packed + pltpu.roll(pair, 4 * vloc * k, 1)
    g1_send[...] = packed
    g1_recv[vec * n_col + col] = packed

    def g1_side(d):
        return remote(g1_send, g1_recv.at[vec * n_col + col], o_s, g1_r, {"col": (col + d) % n_col})

    def g1_over(d):
        return remote(
            g1_send, g1_recv.at[vec * n_col + col], o_s, g1_r,
            {"col": (col + d) % n_col, "vec": oth},
        )

    for d in range(n_col):
        g1_over(d).start()
    for d in range(1, n_col):
        g1_side(d).start()
    for d in range(1, n_col):
        r_send(d).start()

    bytes_of(g1_recv.at[pl.ds(0, 2 * n_col - 1)], g1_r)
    own = g1_recv[vec * n_col]
    other = g1_recv[oth * n_col]
    for d in range(1, n_col):
        own = own + g1_recv[vec * n_col + d]
        other = other + g1_recv[oth * n_col + d]
    both = jnp.concatenate([own, other], 0)
    g2_send[...] = both
    g2_recv[row] = both

    def g2(d):
        return remote(g2_send, g2_recv.at[row], o_s, g2_r, {"row": (row + d) % n_row})

    order = sorted(range(1, n_row), key=lambda d: -min(d, n_row - d))
    for d in order:
        g2(d).start()

    bytes_of(row_recv.at[pl.ds(0, n_col - 1)], rs_r)
    image = row_part[pl.ds(pl.multiple_of(col * blk, blk), blk), :] + z_acc[z_block(z), :]
    for d in range(1, n_col):
        image = image + row_recv[(col + d) % n_col]
    acc[...] = image
    by_z(z_recv, 1, lambda k: n_z - 1 - k, zs_r)
    for d in range(n_z - 1, 0, -1):
        @pl.when(z + d < n_z)
        def _():
            acc[...] += z_recv[(z + d) % n_z]

    for m in range(ch):
        prod_ref[:, m * tile:(m + 1) * tile] = acc[m * vloc:(m + 1) * vloc, :].astype(BF16)

    bytes_of(g2_recv.at[pl.ds(0, n_row - 1)], g2_r)
    total = g2_recv[0]
    for d in range(1, n_row):
        total = total + g2_recv[d]

    def unpack(q):
        lines = [total[q:q + 2]] + [pltpu.roll(total[q:q + 2], tile - 4 * vloc * k, 1) for k in range(1, fold)]
        return jnp.concatenate([lines[k][p:p + 1] for p in range(2) for k in range(fold)], 0)

    mine = unpack(0)
    theirs = unpack(2)
    g_own = mine[:, 2 * vloc:3 * vloc] + jnp.transpose(mine)[:vloc, :vloc]
    g_oth = mine[:, 3 * vloc:4 * vloc] + jnp.transpose(theirs)[vloc:2 * vloc, :vloc]
    first = jnp.where(vec == 0, g_own, g_oth)
    second = jnp.where(vec == 0, g_oth, g_own)
    gram_ref[...] = jnp.concatenate([first, second], 1) * scale

    x_sends = n_z + 2 * n_col - 1
    bytes_of(upper.at[pl.ds(0, x_sends * blk // 2)], x_s)
    by_z(upper, blk, lambda k: 2 * k + 1, z_s)
    bytes_of(upper.at[pl.ds(0, (n_col - 1) * blk + (2 * n_col - 1) * 2 + (n_row - 1) * 4)], o_s)


def shards(n_row, n_col, vectors, tile_vals, tile_rows, tile_cols, tile_counts):
    vloc, width = vectors.shape
    slots, tile = tile_vals.shape[2], tile_vals.shape[3]
    ch = width // tile
    blk = ch * vloc
    n_z = n_row // 2
    dma = pltpu.SemaphoreType.DMA
    vmem = functools.partial(pl.BlockSpec, memory_space=pltpu.VMEM)
    scale = 1.0 / math.sqrt(width * n_row * n_col)
    counted = pltpu.with_memory_space_constraint(jnp.pad(tile_counts, ((0, 0), (0, tile - 1))), pltpu.VMEM)
    product, gram = pl.pallas_call(
        functools.partial(kernel, n_row, n_col, scale),
        out_shape=(
            pltpu.VMEM((vloc, width), BF16),
            pltpu.VMEM((vloc, 2 * vloc), F32),
        ),
        in_specs=[vmem()] + [pl.BlockSpec(memory_space=pltpu.HBM)] * 4,
        out_specs=(vmem(), vmem()),
        scratch_shapes=[
            pltpu.SMEM((1, 1, slots), jnp.int32),
            pltpu.SMEM((1, 1, slots), jnp.int32),
            pltpu.VMEM((1, 1, slots), jnp.int32),
            pltpu.VMEM((1, 1, slots), jnp.int32),
            pltpu.VMEM((slots, tile, tile), BF16),
            pltpu.VMEM((ch, vloc, tile), BF16),
            pltpu.VMEM((n_col * ch, vloc, tile), BF16),
            pltpu.VMEM((n_col * ch, vloc, tile), BF16),
            pltpu.VMEM((n_row * ch, vloc, tile), BF16),
            pltpu.VMEM((slots * vloc, tile), F32),
            pltpu.VMEM((slots * vloc, tile), F32),
            pltpu.VMEM((n_row * blk, tile), F32),
            pltpu.VMEM((n_z * blk, tile), F32),
            pltpu.VMEM((n_z * blk, tile), F32),
            pltpu.VMEM((n_z, blk, tile), F32),
            pltpu.VMEM(((n_col + 2) * blk, tile), F32),
            pltpu.VMEM((n_col, blk, tile), F32),
            pltpu.VMEM((blk, tile), F32),
            pltpu.VMEM((2, tile), F32),
            pltpu.VMEM((2 * n_col, 2, tile), F32),
            pltpu.VMEM((4, tile), F32),
            pltpu.VMEM((n_row, 4, tile), F32),
            dma((4,)), *([dma(())] * 14),
        ],
        compiler_params=pltpu.CompilerParams(
            collective_id=0, has_side_effects=True, vmem_limit_bytes=60 * 1024 * 1024
        ),
    )(counted, tile_rows, tile_cols, vectors, tile_vals)
    return product, gram.T


def solution(mesh):
    return jax.shard_map(
        functools.partial(shards, mesh.shape["row"], mesh.shape["col"]),
        mesh=mesh,
        in_specs=(
            P("vec", ("row", "col")),
            P("row", "col", None, None, None),
            P("row", "col", None),
            P("row", "col", None),
            P("row", "col"),
        ),
        out_specs=(P("vec", ("row", "col")), P(None, "vec")),
        check_vma=False,
    )
```

time: 36.6 us -> 33.5 us (0.915)
  Pallas kernels: 34 us -> 31 us
    pallas_call x1, Pallas kernels: 34 us -> 31 us  [shards(): pl.pallas_call(functools.partial(kernel, n_row, n_col, scale), out_shape=...]
where the time goes in v3:
time: 33.5 us
  Pallas kernels  31 us (93%)
  between operations  1.29 us (4%)
  local copies, waits for them, and re-layouts  1.21 us (4%)
    pallas_call x1, Pallas kernels, shards(): pl.pallas_call(functools.partial(kernel, n_row, n_col, scale), out_shape=...  31 us
    unnamed x2, local copies, waits for them, and re-layouts  1.2 us

profile of v3, /device:TPU:1, one launch (start us, length us, event | category | flops | bytes accessed | tf_op | source)
XLA Modules:
  0.0 33.5 jit_solution(4731667424369286955)
XLA Ops:
  1.3 31.0 %shard_map.68 = (bf16[8,1024]{1,0:T(8,128)(2,1)S(1)}, f32[8,16]{1,0:T(8,128)S(1)}) custom-call(s32[1,128]{1,0:T(1,128)S(1)} %pad.4.count_v, s32[1,1,256]{2,1,0:T(1,128)} %rows_hbm.1, s32[1,1,256]{2,1,0:T(1,128)} %cols_hbm.1, bf16[8,1024]{1,0:T(8,128)(2,1)} %x_ref.1, bf16[1,1,256,128,128]{4,3,2,1,0:T(8,128)(2,1)} %tiles_hbm.1), custom_call_target="tpu_custom_call" | custom-call | tf_op jit(solution)/shard_map/pallas_call | solution.py:357
  32.3 0.6 %copy.9 = bf16[8,1024]{1,0:T(8,128)(2,1)} copy(bf16[8,1024]{1,0:T(8,128)(2,1)S(1)} %get-tuple-element.6) | data formatting | bytes 32768
  32.9 0.6 %copy.10 = f32[16,8]{0,1:T(8,128)} copy(f32[16,8]{0,1:T(8,128)S(1)} %bitcast.1) | data formatting | bytes 1024
  (1 shorter events, 0.0 us)

commit v4 on v3

--- a/solution.py
+++ b/solution.py
@@ -26,7 +26,7 @@
     prod_ref, gram_ref,
     rows_s, cols_s, rows_v, cols_v, tiles, x_mine, x_row, x_oth, x_col, upper, down, col_part, exch, z_acc, z_recv, row_part, row_recv, acc,
     g1_send, g1_recv, g2_send, g2_recv,
-    list_sem, mine_sem, tile_sem, x_s, xz_r, xf_r, xr_r, xo_r, z_s, ex_r, zs_r, o_s, rs_r, g1_r, g2_r,
+    list_sem, mine_sem, tile_sem, x_s, xz_r, xf_r, xr_r, xp_r, xo_r, z_s, ex_r, zs_r, o_s, rs_r, g1_r, g2_r,
 ):
     n_z = n_row // 2
     slots = tiles.shape[0]
@@ -92,10 +92,12 @@
     def x_side(d):
         return remote(x_mine, x_row.at[owned(col)], x_s, xr_r, {"col": (col + d) % n_col})
 
-    def x_over(d):
-        return remote(
-            x_mine, x_oth.at[owned(col)], x_s, xo_r, {"col": (col + d) % n_col, "vec": oth}
-        )
+    def x_over():
+        return remote(x_mine, x_oth.at[owned(col)], x_s, xp_r, {"vec": oth})
+
+    def x_pass(d):
+        part = x_oth.at[owned(col)]
+        return remote(part, part, x_s, xo_r, {"col": (col + d) % n_col})
 
     for d in far:
         @pl.when(z + d < n_z)
@@ -103,6 +105,7 @@
             x_up(d).start()
     for d in range(1, n_col):
         x_side(d).start()
+    x_over().start()
     x_row[owned(col)] = x_mine[...]
     x_col[owned(row)] = x_mine[...]
     for k in range(2, n_row):
@@ -137,8 +140,9 @@
                     bytes_of(ref.at[pl.ds(0, count(k) * unit)], sem)
 
     bytes_of(x_row.at[pl.ds(0, (n_col - 1) * ch)], xr_r)
-    for d in range(n_col):
-        x_over(d).start()
+    bytes_of(x_oth.at[owned(col)], xp_r)
+    for d in range(1, n_col):
+        x_pass(d).start()
 
     zero = jnp.zeros((vloc, tile), BF16)
 
@@ -162,7 +166,7 @@
         return x_col[lax.shift_right_logical(c, span_bits) * ch + (c & (ch - 1))]
 
     bytes_of(tiles, tile_sem)
-    for t in range(0, slots // 2, 2):
+    for t in range(0, 3 * slots // 4, 2):
         two(pick_row, t, upper, False)
 
     by_z(x_col, ch, lambda k: k, xz_r)
@@ -171,7 +175,7 @@
         def _():
             x_forward(z - d).start()
 
-    for t in range(slots // 2, slots, 2):
+    for t in range(3 * slots // 4, slots, 2):
         two(pick_row, t, upper, False)
 
     def scatter(src, hot, dst):
@@ -216,7 +220,7 @@
         )
 
     for t in range(0, slots, 2):
-        if t == slots // 4:
+        if t == slots // 2:
             by_z(exch, blk, lambda k: k + 1, ex_r)
             for d in near:
                 @pl.when(z - d >= 0)
@@ -243,7 +247,7 @@
             {"col": to},
         )
 
-    bytes_of(x_oth, xo_r)
+    bytes_of(x_oth.at[pl.ds(0, (n_col - 1) * ch)], xo_r)
 
     def against(base, j):
         part = jnp.concatenate(
@@ -342,6 +346,15 @@
     bytes_of(upper.at[pl.ds(0, x_sends * blk // 2)], x_s)
     by_z(upper, blk, lambda k: 2 * k + 1, z_s)
     bytes_of(upper.at[pl.ds(0, (n_col - 1) * blk + (2 * n_col - 1) * 2 + (n_row - 1) * 4)], o_s)
+
+
+def hand_over(prod_ref, gram_ref, prod_out, gram_out, sem):
+    one = pltpu.make_async_copy(prod_ref, prod_out, sem.at[0])
+    two = pltpu.make_async_copy(gram_ref, gram_out, sem.at[1])
+    one.start()
+    two.start()
+    one.wait()
+    two.wait()
 
 
 def shards(n_row, n_col, vectors, tile_vals, tile_rows, tile_cols, tile_counts):
@@ -385,12 +398,22 @@
             pltpu.VMEM((2 * n_col, 2, tile), F32),
             pltpu.VMEM((4, tile), F32),
             pltpu.VMEM((n_row, 4, tile), F32),
-            dma((4,)), *([dma(())] * 14),
+            dma((4,)), *([dma(())] * 15),
         ],
         compiler_params=pltpu.CompilerParams(
             collective_id=0, has_side_effects=True, vmem_limit_bytes=60 * 1024 * 1024
         ),
     )(counted, tile_rows, tile_cols, vectors, tile_vals)
+    product, gram = pl.pallas_call(
+        hand_over,
+        out_shape=(
+            jax.ShapeDtypeStruct((vloc, width), BF16),
+            jax.ShapeDtypeStruct((vloc, 2 * vloc), F32),
+        ),
+        in_specs=[vmem(), vmem()],
+        out_specs=(pl.BlockSpec(memory_space=pl.ANY), pl.BlockSpec(memory_space=pl.ANY)),
+        scratch_shapes=[dma((2,))],
+    )(pltpu.with_memory_space_constraint(product, pltpu.VMEM), pltpu.with_memory_space_constraint(gram, pltpu.VMEM))
     return product, gram.T
 
 

time: 33.5 us -> 32.6 us (0.973)
  local copies, waits for them, and re-layouts: 1.21 us -> 0.01 us
    unnamed x2 -> x0, local copies, waits for them, and re-layouts: 1.2 us -> none
    pallas_call x0 -> x1, Pallas kernels: none -> 0.63 us  [shards(): pl.pallas_call(hand_over, out_shape=(jax.ShapeDtypeStruct((vloc, width),...]
    pallas_call x1, Pallas kernels: 31 us -> 30.6 us  [shards(): pl.pallas_call(functools.partial(kernel, n_row, n_col, scale), out_shape=...]
where the time goes in v4:
time: 32.6 us; the launch traced here: 32.5 us
  Pallas kernels  31.2 us (96%)
  between operations  1.29 us (4%)
    pallas_call x1, Pallas kernels, shards(): pl.pallas_call(functools.partial(kernel, n_row, n_col, scale), out_shape=...  30.6 us

profile of v4, /device:TPU:1, one launch (start us, length us, event | category | flops | bytes accessed | tf_op | source)
XLA Modules:
  0.0 32.5 jit_solution(16940025763093432029)
XLA Ops:
  1.3 30.6 %shard_map.68 = (bf16[8,1024]{1,0:T(8,128)(2,1)S(1)}, f32[8,16]{1,0:T(8,128)S(1)}) custom-call(s32[1,128]{1,0:T(1,128)S(1)} %pad.4.count_v, s32[1,1,256]{2,1,0:T(1,128)} %rows_hbm.1, s32[1,1,256]{2,1,0:T(1,128)} %cols_hbm.1, bf16[8,1024]{1,0:T(8,128)(2,1)} %x_ref.1, bf16[1,1,256,128,128]{4,3,2,1,0:T(8,128)(2,1)} %tiles_hbm.1), custom_call_target="tpu_custom_call" | custom-call | tf_op jit(solution)/shard_map/pallas_call | solution.py:370
  31.9 0.6 %shard_map.69 = (bf16[8,1024]{1,0:T(8,128)(2,1)}, f32[8,16]{1,0:T(8,128)}) custom-call(bf16[8,1024]{1,0:T(8,128)(2,1)S(1)} %get-tuple-element.6.prod_ref, f32[8,16]{1,0:T(8,128)S(1)} %get-tuple-element.7.gram_ref), custom_call_target="tpu_custom_call" | custom-call | tf_op jit(solution)/shard_map/pallas_call | solution.py:407
  (1 shorter events, 0.0 us)

commit v5 on v4

--- a/solution.py
+++ b/solution.py
@@ -166,7 +166,7 @@
         return x_col[lax.shift_right_logical(c, span_bits) * ch + (c & (ch - 1))]
 
     bytes_of(tiles, tile_sem)
-    for t in range(0, 3 * slots // 4, 2):
+    for t in range(0, slots, 2):
         two(pick_row, t, upper, False)
 
     by_z(x_col, ch, lambda k: k, xz_r)
@@ -175,7 +175,7 @@
         def _():
             x_forward(z - d).start()
 
-    for t in range(3 * slots // 4, slots, 2):
+    for t in range(slots, slots, 2):
         two(pick_row, t, upper, False)
 
     def scatter(src, hot, dst):
@@ -220,16 +220,17 @@
         )
 
     for t in range(0, slots, 2):
-        if t == slots // 2:
-            by_z(exch, blk, lambda k: k + 1, ex_r)
-            for d in near:
-                @pl.when(z - d >= 0)
-                def _():
-                    keep = pl.ds(pl.multiple_of(core * half + (z - d) * blk, blk), blk)
-                    z_acc[z_block(z - d), :] = col_part[keep, :] + exch[z_block(z - d), :]
-                    if d:
-                        z_send(d).start()
         two(pick_col, t, down, True)
+
+    by_z(exch, blk, lambda k: k + 1, ex_r)
+    for d in near:
+        @pl.when(z - d >= 0)
+        def _():
+            keep = pl.ds(pl.multiple_of(core * half + (z - d) * blk, blk), blk)
+            z_acc[z_block(z - d), :] = col_part[keep, :] + exch[z_block(z - d), :]
+            if d:
+                z_send(d).start()
+
 
     row_hot = jnp.concatenate(
         [

time: 32.6 us -> 32.2 us (0.988)
    pallas_call x1, Pallas kernels: 30.6 us -> 30.2 us  [shards(): pl.pallas_call(functools.partial(kernel, n_row, n_col, scale), out_shape=...]
where the time goes in v5:
time: 32.2 us; the launch traced here: 32.1 us
  Pallas kernels  30.9 us (96%)
  between operations  1.29 us (4%)
    pallas_call x1, Pallas kernels, shards(): pl.pallas_call(functools.partial(kernel, n_row, n_col, scale), out_shape=...  30.2 us

profile of v5, /device:TPU:1, one launch (start us, length us, event | category | flops | bytes accessed | tf_op | source)
XLA Modules:
  0.0 32.1 jit_solution(3578146778286003677)
XLA Ops:
  1.3 30.2 %shard_map.68 = (bf16[8,1024]{1,0:T(8,128)(2,1)S(1)}, f32[8,16]{1,0:T(8,128)S(1)}) custom-call(s32[1,128]{1,0:T(1,128)S(1)} %pad.4.count_v, s32[1,1,256]{2,1,0:T(1,128)} %rows_hbm.1, s32[1,1,256]{2,1,0:T(1,128)} %cols_hbm.1, bf16[8,1024]{1,0:T(8,128)(2,1)} %x_ref.1, bf16[1,1,256,128,128]{4,3,2,1,0:T(8,128)(2,1)} %tiles_hbm.1), custom_call_target="tpu_custom_call" | custom-call | tf_op jit(solution)/shard_map/pallas_call | solution.py:371
  31.5 0.6 %shard_map.69 = (bf16[8,1024]{1,0:T(8,128)(2,1)}, f32[8,16]{1,0:T(8,128)}) custom-call(bf16[8,1024]{1,0:T(8,128)(2,1)S(1)} %get-tuple-element.6.prod_ref, f32[8,16]{1,0:T(8,128)S(1)} %get-tuple-element.7.gram_ref), custom_call_target="tpu_custom_call" | custom-call | tf_op jit(solution)/shard_map/pallas_call | solution.py:408
  (1 shorter events, 0.0 us)

commit v6 on v5

--- a/solution.py
+++ b/solution.py
@@ -24,7 +24,7 @@
     n_row, n_col, scale,
     count_v, rows_hbm, cols_hbm, x_ref, tiles_hbm,
     prod_ref, gram_ref,
-    rows_s, cols_s, rows_v, cols_v, tiles, x_mine, x_row, x_oth, x_col, upper, down, col_part, exch, z_acc, z_recv, row_part, row_recv, acc,
+    rows_s, cols_s, rows_v, cols_v, tiles, flipped, x_mine, x_row, x_oth, x_col, upper, down, col_part, exch, z_acc, z_recv, row_part, row_recv, acc,
     g1_send, g1_recv, g2_send, g2_recv,
     list_sem, mine_sem, tile_sem, x_s, xz_r, xf_r, xr_r, xp_r, xo_r, z_s, ex_r, zs_r, o_s, rs_r, g1_r, g2_r,
 ):
@@ -99,13 +99,13 @@
         part = x_oth.at[owned(col)]
         return remote(part, part, x_s, xo_r, {"col": (col + d) % n_col})
 
+    x_over().start()
     for d in far:
         @pl.when(z + d < n_z)
         def _():
             x_up(d).start()
     for d in range(1, n_col):
         x_side(d).start()
-    x_over().start()
     x_row[owned(col)] = x_mine[...]
     x_col[owned(row)] = x_mine[...]
     for k in range(2, n_row):
@@ -139,14 +139,23 @@
                 def _():
                     bytes_of(ref.at[pl.ds(0, count(k) * unit)], sem)
 
+    bytes_of(tiles, tile_sem)
+
+    def flip(c, carry):
+        for q in range(per):
+            flipped[c * per + q] = jnp.transpose(tiles[c * per + q])
+        return carry
+
+    lax.fori_loop(0, CHUNKS, flip, 0)
+
+    bytes_of(x_oth.at[owned(col)], xp_r)
+    for d in range(1, n_col):
+        x_pass(d).start()
     bytes_of(x_row.at[pl.ds(0, (n_col - 1) * ch)], xr_r)
-    bytes_of(x_oth.at[owned(col)], xp_r)
-    for d in range(1, n_col):
-        x_pass(d).start()
 
     zero = jnp.zeros((vloc, tile), BF16)
 
-    def two(pick, first, out, trans):
+    def two(pick, first, out, held):
         left = jnp.concatenate(
             [
                 jnp.concatenate([pick(first), zero], 1),
@@ -154,9 +163,8 @@
             ],
             0,
         )
-        w = jnp.concatenate([tiles[first], tiles[first + 1]], 1 if trans else 0)
-        dims = (((1,), (1 if trans else 0,)), ((), ()))
-        out[first * vloc:(first + 2) * vloc, :] = lax.dot_general(left, w, dims, preferred_element_type=F32)
+        w = jnp.concatenate([held[first], held[first + 1]], 0)
+        out[first * vloc:(first + 2) * vloc, :] = jnp.dot(left, w, preferred_element_type=F32)
 
     def pick_row(t):
         return x_row[rows_s[0, 0, t] & (span - 1)]
@@ -165,9 +173,8 @@
         c = cols_s[0, 0, t]
         return x_col[lax.shift_right_logical(c, span_bits) * ch + (c & (ch - 1))]
 
-    bytes_of(tiles, tile_sem)
     for t in range(0, slots, 2):
-        two(pick_row, t, upper, False)
+        two(pick_row, t, upper, tiles)
 
     by_z(x_col, ch, lambda k: k, xz_r)
     for d in far:
@@ -176,7 +183,7 @@
             x_forward(z - d).start()
 
     for t in range(slots, slots, 2):
-        two(pick_row, t, upper, False)
+        two(pick_row, t, upper, tiles)
 
     def scatter(src, hot, dst):
         m = hot.shape[0]
@@ -220,7 +227,7 @@
         )
 
     for t in range(0, slots, 2):
-        two(pick_col, t, down, True)
+        two(pick_col, t, down, flipped)
 
     by_z(exch, blk, lambda k: k + 1, ex_r)
     for d in near:
@@ -381,6 +388,7 @@
             pltpu.SMEM((1, 1, slots), jnp.int32),
             pltpu.VMEM((1, 1, slots), jnp.int32),
             pltpu.VMEM((1, 1, slots), jnp.int32),
+            pltpu.VMEM((slots, tile, tile), BF16),
             pltpu.VMEM((slots, tile, tile), BF16),
             pltpu.VMEM((ch, vloc, tile), BF16),
             pltpu.VMEM((n_col * ch, vloc, tile), BF16),

time: 32.2 us -> 31.6 us (0.981)
  Pallas kernels: 30.9 us -> 30.2 us
    pallas_call x1, Pallas kernels: 30.2 us -> 29.6 us  [shards(): pl.pallas_call(functools.partial(kernel, n_row, n_col, scale), out_shape=...]
where the time goes in v6:
time: 31.6 us; the launch traced here: 31.5 us
  Pallas kernels  30.2 us (96%)
  between operations  1.29 us (4%)
    pallas_call x1, Pallas kernels, shards(): pl.pallas_call(functools.partial(kernel, n_row, n_col, scale), out_shape=...  29.6 us

profile of v6, /device:TPU:1, one launch (start us, length us, event | category | flops | bytes accessed | tf_op | source)
XLA Modules:
  0.0 31.5 jit_solution(3904741426511846550)
XLA Ops:
  1.3 29.6 %shard_map.68 = (bf16[8,1024]{1,0:T(8,128)(2,1)S(1)}, f32[8,16]{1,0:T(8,128)S(1)}) custom-call(s32[1,128]{1,0:T(1,128)S(1)} %pad.4.count_v, s32[1,1,256]{2,1,0:T(1,128)} %rows_hbm.1, s32[1,1,256]{2,1,0:T(1,128)} %cols_hbm.1, bf16[8,1024]{1,0:T(8,128)(2,1)} %x_ref.1, bf16[1,1,256,128,128]{4,3,2,1,0:T(8,128)(2,1)} %tiles_hbm.1), custom_call_target="tpu_custom_call" | custom-call | tf_op jit(solution)/shard_map/pallas_call | solution.py:378
  30.9 0.6 %shard_map.69 = (bf16[8,1024]{1,0:T(8,128)(2,1)}, f32[8,16]{1,0:T(8,128)}) custom-call(bf16[8,1024]{1,0:T(8,128)(2,1)S(1)} %get-tuple-element.6.prod_ref, f32[8,16]{1,0:T(8,128)S(1)} %get-tuple-element.7.gram_ref), custom_call_target="tpu_custom_call" | custom-call | tf_op jit(solution)/shard_map/pallas_call | solution.py:416
  (1 shorter events, 0.0 us)

commit v7 on v6

--- a/solution.py
+++ b/solution.py
@@ -11,7 +11,7 @@
 MESH = pl.DeviceIdType.MESH
 BF16 = jnp.bfloat16
 F32 = jnp.float32
-CHUNKS = 8
+CHUNKS = 4
 
 
 def split_hi_lo(value):

time: 31.6 us -> 31.6 us (level)
  no operation moved by 1% of the time
where the time goes in v7:
time: 31.6 us; the launch traced here: 31.5 us
  Pallas kernels  30.2 us (96%)
  between operations  1.29 us (4%)
    pallas_call x1, Pallas kernels, shards(): pl.pallas_call(functools.partial(kernel, n_row, n_col, scale), out_shape=...  29.6 us

profile of v7, /device:TPU:1, one launch (start us, length us, event | category | flops | bytes accessed | tf_op | source)
XLA Modules:
  0.0 31.5 jit_solution(14906947142455841658)
XLA Ops:
  1.3 29.6 %shard_map.68 = (bf16[8,1024]{1,0:T(8,128)(2,1)S(1)}, f32[8,16]{1,0:T(8,128)S(1)}) custom-call(s32[1,128]{1,0:T(1,128)S(1)} %pad.4.count_v, s32[1,1,256]{2,1,0:T(1,128)} %rows_hbm.1, s32[1,1,256]{2,1,0:T(1,128)} %cols_hbm.1, bf16[8,1024]{1,0:T(8,128)(2,1)} %x_ref.1, bf16[1,1,256,128,128]{4,3,2,1,0:T(8,128)(2,1)} %tiles_hbm.1), custom_call_target="tpu_custom_call" | custom-call | tf_op jit(solution)/shard_map/pallas_call | solution.py:378
  30.9 0.6 %shard_map.69 = (bf16[8,1024]{1,0:T(8,128)(2,1)}, f32[8,16]{1,0:T(8,128)}) custom-call(bf16[8,1024]{1,0:T(8,128)(2,1)S(1)} %get-tuple-element.6.prod_ref, f32[8,16]{1,0:T(8,128)S(1)} %get-tuple-element.7.gram_ref), custom_call_target="tpu_custom_call" | custom-call | tf_op jit(solution)/shard_map/pallas_call | solution.py:416
  (1 shorter events, 0.0 us)
